TPU v7x, 256 devices: a whole 4x4x8 slice. The times are simulated.
256 devices in a mesh: dp: 16 (over z_hi, x, core), fsdp: 16 (over z_lo, y).
Axes of the slice: x: 4, y: 4, z: 8 (z_hi: 2, z_lo: 4; z = z_hi * 4 + z_lo), core: 2. Of those that a mesh axis runs over, the one named last changes fastest.
Arguments:
- attn_heads: bfloat16 [512, 4096], P('dp', 'fsdp'), may hold values from -6 to 6
- out_proj: bfloat16 [4096, 4608], P('fsdp'), may hold values from -0.09375 to 0.09375
- resid_pre: bfloat16 [512, 4608], P(('dp', 'fsdp')), may hold values from -25 to 25
- post_gain: float32 [4608], replicated, may hold values from 0.5 to 1.5
- enc_weight: bfloat16 [4608, 65536], P(None, ('dp', 'fsdp')), may hold values from -0.09375 to 0.09375
- enc_bias: float32 [65536], P(('dp', 'fsdp')), may hold values from -3 to 3
- dec_weight: bfloat16 [65536, 4608], P(('dp', 'fsdp')), may hold values from -0.046875 to 0.046875
- dec_bias: float32 [4608], replicated, may hold values from -3 to 3
Outputs:
- enc_grad: bfloat16 [4608, 65536], P(None, ('dp', 'fsdp'))
- enc_bias_grad: float32 [65536], P(('dp', 'fsdp'))
- dec_grad: bfloat16 [65536, 4608], P(('dp', 'fsdp'))
- dec_bias_grad: float32 [4608], replicated
- loss: float32 [], replicated
All inputs are finite; a program needn't handle non-finite values.
Results may differ from a plain program's by a relative error of at most 0.013.
Values may be sent and summed in bfloat16 or wider, within the bound.
A program may use at most 128 MiB of HBM per device.

v0:
```python
import jax
import jax.numpy as jnp
from jax import lax
from jax.sharding import PartitionSpec as P

SPARSITY = 0.25
SMOOTHING = 0.1
EPSILON = 1e-06


def finish(summed, resid_rows, post_gain):
    scale = lax.rsqrt(jnp.mean(summed * summed, axis=-1, keepdims=True) + EPSILON)
    return (resid_rows.astype(jnp.float32) + summed * scale * post_gain).astype(jnp.bfloat16)


def body(attn_heads, out_proj, resid_pre, post_gain, enc_weight, enc_bias, dec_weight, dec_bias):
    block = attn_heads
    summed = lax.psum_scatter(
        jnp.dot(block, out_proj, preferred_element_type=jnp.float32),
        "fsdp",
        scatter_dimension=0,
        tiled=True,
    )
    resid_own = finish(summed, resid_pre, post_gain)
    resid_all = lax.all_gather(resid_own, ("dp", "fsdp"), axis=0, tiled=True)
    preact = jnp.dot(resid_all, enc_weight, preferred_element_type=jnp.float32) + enc_bias
    latents = jnp.maximum(preact, 0.0)
    latents_b = latents.astype(jnp.bfloat16)
    row_norms = jnp.sqrt(jnp.sum(jnp.square(dec_weight.astype(jnp.float32)), axis=1) + EPSILON)
    penalty_local = jnp.sum(latents * row_norms)
    penalty_total = lax.psum(penalty_local, ("dp", "fsdp"))
    block = latents_b
    recon = lax.psum_scatter(
        jnp.dot(block, dec_weight, preferred_element_type=jnp.float32),
        ("dp", "fsdp"),
        scatter_dimension=0,
        tiled=True,
    )
    recon = recon + dec_bias
    error = recon - resid_own.astype(jnp.float32)
    error_local = jnp.sum(error * error)
    error_total = lax.psum(error_local, ("dp", "fsdp"))
    loss = (0.5 * error_total + SPARSITY * penalty_total) / (
        resid_all.shape[0] * resid_all.shape[1]
    )
    error_b = error.astype(jnp.bfloat16)
    error_all = lax.all_gather(error_b, ("dp", "fsdp"), axis=0, tiled=True)
    dec_bias_grad = jnp.sum(error_all, axis=0, dtype=jnp.float32)
    usage = jnp.sum(latents, axis=0)
    dec_grad = lax.dot_general(
        latents_b, error_all, (((0,), (0,)), ((), ())), preferred_element_type=jnp.float32
    )
    dec_grad = (
        dec_grad + SPARSITY * (usage / row_norms)[:, None] * dec_weight.astype(jnp.float32)
    ).astype(jnp.bfloat16)
    latent_grad = lax.dot_general(
        error_all, dec_weight, (((1,), (1,)), ((), ())), preferred_element_type=jnp.float32
    )
    latent_grad = latent_grad + SPARSITY * row_norms
    preact_grad = latent_grad * jax.nn.sigmoid(preact / SMOOTHING)
    enc_bias_grad = jnp.sum(preact_grad, axis=0)
    enc_grad = lax.dot_general(
        resid_all,
        preact_grad.astype(jnp.bfloat16),
        (((0,), (0,)), ((), ())),
        preferred_element_type=jnp.float32,
    ).astype(jnp.bfloat16)
    return (enc_grad, enc_bias_grad, dec_grad, dec_bias_grad, loss)


def solution(mesh):
    placed = (
        P("dp", "fsdp"),
        P("fsdp", None),
        P(("dp", "fsdp"), None),
        P(),
        P(None, ("dp", "fsdp")),
        P(("dp", "fsdp")),
        P(("dp", "fsdp"), None),
        P(),
    )
    return jax.shard_map(
        body,
        mesh=mesh,
        in_specs=placed,
        out_specs=(P(None, ("dp", "fsdp")), P(("dp", "fsdp")), P(("dp", "fsdp"), None), P(), P()),
        check_vma=False,
    )
```

profile of v0, /device:TPU:99, one launch (start us, length us, event | category | flops | bytes accessed | tf_op | source)
XLA Modules:
  0.0 1927.3 jit_solution(9511033964533940527)
XLA Ops:
  7.2 0.0 copy-start
  7.2 0.0 all-reduce.6.cloned.1.call-start
  7.2 1.6 copy-done
  8.8 2.0 fusion.9
  10.9 0.0 all-reduce.6.cloned.1.call-update
  10.9 0.0 all-gather.5.cloned.1.call-start
  11.0 1.3 dynamic-slice
  12.9 144.5 %all-reduce.6.cloned.1.call-done = f32[32,4608]{1,0:T(8,128)} async-done(((f32[32,4608]{1,0:T(8,128)}), f32[32,4608]{1,0:T(8,128)}) %all-reduce.6.cloned.1.call-update) | async-done | bytes 589840
  157.3 1.1 multiply_reduce_fusion.2
  158.4 1.6 add_convert_fusion
  160.0 0.0 all-gather.5.cloned.1.call-update
  160.1 0.0 all-reduce.8.cloned.1.call-start
  160.1 2.2 fusion.1
  162.3 0.0 copy-start.6
  162.3 727.9 %all-gather.5.cloned.1.call-done = bf16[256,2,4608]{2,1,0:T(2,128)(2,1)} async-done(((bf16[1,2,4608]{2,1,0:T(2,128)(2,1)}), bf16[256,2,4608]{2,1,0:T(2,128)(2,1)}) %all-gather.5.cloned.1.call-update) | async-done | bytes 4718608 | tf_op jit(solution)/shard_map/all_gather | solution.py:25
  890.2 7.6 reshape.38
  897.8 0.0 copy-done.6
  897.8 0.0 copy-start.2
  897.8 5.2 multiply_reduce_fusion
  903.0 0.0 copy-done.2
  903.0 5.1 fusion.4
  908.1 0.0 copy-start.4
  908.1 0.0 copy-start.5
  908.1 0.0 all-reduce.8.cloned.1.call-update
  908.1 0.0 all-gather.7.cloned.1.call-start
  908.1 275.0 %all-reduce.8.cloned.1.call-done = f32[512,4608]{1,0:T(8,128)} async-done(((f32[512,4608]{1,0:T(8,128)}), f32[512,4608]{1,0:T(8,128)}) %all-reduce.8.cloned.1.call-update) | async-done | bytes 9437200
  1183.1 0.0 copy-done.4
  1183.1 0.0 copy-done.5
  1183.1 2.2 multiply_reduce_fusion.1
  1185.3 0.0 all-gather.7.cloned.1.call-update
  1185.3 72.2 %all-reduce.2 = (f32[]{:T(128)}, f32[]{:T(128)}) all-reduce(f32[]{:T(128)} %get-tuple-element.9, f32[]{:T(128)} %get-tuple-element.5), channel_id=1, replica_groups=mesh['dp'=16,'fsdp'=16] {'dp','fsdp'}, use_global_device_ids=true, to_apply=%region_8.0 | all-reduce | flops 2 | bytes 16 | tf_op jit(solution)/shard_map/psum | solution.py:42
  1258.8 639.6 %all-gather.7.cloned.1.call-done = bf16[256,2,4608]{2,1,0:T(2,128)(2,1)} async-done(((bf16[1,2,4608]{2,1,0:T(2,128)(2,1)}), bf16[256,2,4608]{2,1,0:T(2,128)(2,1)}) %all-gather.7.cloned.1.call-update) | async-done | bytes 4718608 | tf_op jit(solution)/shard_map/all_gather | solution.py:47
  1898.4 7.6 reshape.40
  1906.0 0.0 copy-start.1
  1906.0 0.0 slice-start
  1906.0 4.1 convert_reduce_fusion
  1910.1 0.0 copy-done.1
  1910.1 0.0 copy-start.3
  1910.1 0.0 slice-start.1
  1910.1 3.8 fusion.8
  1913.9 0.0 copy-done.3
  1913.9 2.9 fusion
  1916.7 0.0 slice-done
  1916.7 0.0 slice-done.1
  1916.8 2.9 convolution_convert_fusion
  (4 shorter events, 0.0 us)
Async XLA Ops:
  7.2 1.7 copy-start
  7.2 150.2 %all-reduce.6.cloned.1.call-start = ((), (), s32[]{:S(2)}) async-start(), calls=%async_computation.2 | async-start | bytes 1179648
  10.9 879.3 %all-gather.5.cloned.1.call-start = ((), (), s32[]{:S(2)}) async-start(), calls=%async_computation | async-start | bytes 4737024 | tf_op jit(solution)/shard_map/all_gather | solution.py:25
  160.1 1023.0 %all-reduce.8.cloned.1.call-start = ((), (), s32[]{:S(2)}) async-start(), calls=%async_computation.3 | async-start | bytes 18874368
  162.3 735.4 %copy-start.6 = (f32[256]{0:T(256)S(1)}, f32[256]{0:T(256)}, u32[]{:S(2)}) copy-start(f32[256]{0:T(256)} %param.13) | copy-start | bytes 3076
  897.8 5.2 copy-start.2
  908.1 275.0 %copy-start.4 = (bf16[2,4608]{1,0:T(2,128)(2,1)S(1)}, bf16[2,4608]{1,0:T(2,128)(2,1)}, u32[]{:S(2)}) copy-start(bf16[2,4608]{1,0:T(2,128)(2,1)} %add_convert_fusion) | copy-start | bytes 55300
  908.1 275.0 %copy-start.5 = (f32[4608]{0:T(1024)S(1)}, f32[4608]{0:T(1024)}, u32[]{:S(2)}) copy-start(f32[4608]{0:T(1024)} %param.15) | copy-start | bytes 55300
  908.1 990.3 %all-gather.7.cloned.1.call-start = ((), (), s32[]{:S(2)}) async-start(), calls=%async_computation.1 | async-start | bytes 4737024 | tf_op jit(solution)/shard_map/all_gather | solution.py:47
  1906.0 4.1 copy-start.1
  1906.0 10.7 slice-start
  1910.1 3.8 copy-start.3
  1910.1 6.7 slice-start.1
Sparse Core Ops, SparseCore 0:
  11.2 146.0 all-reduce.5
  160.2 729.9 all-gather.4
  908.2 274.8 all-reduce.7
  1185.4 712.9 all-gather.6
where the time goes:
time: 1930 us
  waiting for transfers between devices  1790 us (93%)
  blocking collectives  72.2 us (4%)
  matrix products  21.9 us (1%)
    all_gather x1, waiting for transfers between devices, body(): resid_all = lax.all_gather(resid_own, ('dp', 'fsdp'), axis=0, tiled=True)  728 us
    all_gather x1, waiting for transfers between devices, body(): error_all = lax.all_gather(error_b, ('dp', 'fsdp'), axis=0, tiled=True)  640 us
    unnamed x6, waiting for transfers between devices  419 us
    psum x1, blocking collectives, body(): error_total = lax.psum(error_local, ('dp', 'fsdp'))  72.2 us
  transfers between devices with their start and end apart: 4, of which 4 were waited for; matrix products, arithmetic and copies ran while one was open for 0% of the time, Pallas kernels for 0%

commit v1 on v0

--- a/solution.py
+++ b/solution.py
@@ -44,7 +44,10 @@
         resid_all.shape[0] * resid_all.shape[1]
     )
     error_b = error.astype(jnp.bfloat16)
-    error_all = lax.all_gather(error_b, ("dp", "fsdp"), axis=0, tiled=True)
+    error_all = jnp.concatenate(
+        lax.all_to_all(jnp.stack([error_b] * lax.axis_size(("dp", "fsdp"))), ("dp", "fsdp"), 0, 0),
+        axis=0,
+    )
     dec_bias_grad = jnp.sum(error_all, axis=0, dtype=jnp.float32)
     usage = jnp.sum(latents, axis=0)
     dec_grad = lax.dot_general(

time: 1930 us -> 1380 us (0.72)
  waiting for transfers between devices: 1790 us -> 1150 us
  blocking collectives: 72.2 us -> 146 us
    all_gather x1 -> x0, waiting for transfers between devices: 640 us -> none  [body(): error_all = lax.all_gather(error_b, ('dp', 'fsdp'), axis=0, tiled=True)]
    psum x1, blocking collectives: 72.2 us -> 146 us  [body(): error_total = lax.psum(error_local, ('dp', 'fsdp'))]
    unnamed x6 -> x5, waiting for transfers between devices: 419 us -> 419 us
  transfers between devices with their start and end apart: 4 -> 4, of which waited for: 4 -> 3; matrix products, arithmetic and copies ran while one was open for 0% -> 0% of each run, Pallas kernels for 0% -> 0%
where the time goes in v1:
time: 1380 us
  waiting for transfers between devices  1150 us (83%)
  blocking collectives  146 us (11%)
  matrix products  23.3 us (2%)
  local copies, waits for them, and re-layouts  22.7 us (2%)
  between operations  16.9 us (1%)
    all_gather x1, waiting for transfers between devices, body(): resid_all = lax.all_gather(resid_own, ('dp', 'fsdp'), axis=0, tiled=True)  728 us
    unnamed x5, waiting for transfers between devices  419 us
    psum x1, blocking collectives, body(): error_total = lax.psum(error_local, ('dp', 'fsdp'))  146 us
  transfers between devices with their start and end apart: 4, of which 3 were waited for; matrix products, arithmetic and copies ran while one was open for 0% of the time, Pallas kernels for 0%

profile of v1, /device:TPU:99, one launch (start us, length us, event | category | flops | bytes accessed | tf_op | source)
XLA Modules:
  0.0 1377.8 jit_solution(3137325471463486131)
XLA Ops:
  7.2 0.0 copy-start
  7.2 0.0 all-reduce.6.cloned.1.call-start
  7.2 1.6 copy-done
  8.8 2.0 fusion.10
  10.9 0.0 all-reduce.6.cloned.1.call-update
  10.9 0.0 all-gather.3.cloned.1.call-start
  11.0 1.3 dynamic-slice
  12.9 144.5 %all-reduce.6.cloned.1.call-done = f32[32,4608]{1,0:T(8,128)} async-done(((f32[32,4608]{1,0:T(8,128)}), f32[32,4608]{1,0:T(8,128)}) %all-reduce.6.cloned.1.call-update) | async-done | bytes 589840
  157.3 1.1 multiply_reduce_fusion.2
  158.4 1.6 add_convert_fusion
  160.0 0.0 all-gather.3.cloned.1.call-update
  160.1 0.0 all-reduce.8.cloned.1.call-start
  160.1 2.2 fusion.1
  162.3 0.0 copy-start.6
  162.3 727.9 %all-gather.3.cloned.1.call-done = bf16[256,2,4608]{2,1,0:T(2,128)(2,1)} async-done(((bf16[1,2,4608]{2,1,0:T(2,128)(2,1)}), bf16[256,2,4608]{2,1,0:T(2,128)(2,1)}) %all-gather.3.cloned.1.call-update) | async-done | bytes 4718608 | tf_op jit(solution)/shard_map/all_gather | solution.py:25
  890.2 7.6 reshape.44
  897.8 0.0 copy-done.6
  897.8 0.0 copy-start.1
  897.8 5.2 multiply_reduce_fusion
  903.0 0.0 copy-done.1
  903.0 5.1 fusion.4
  908.1 0.0 copy-start.4
  908.1 0.0 copy-start.5
  908.1 0.0 all-reduce.8.cloned.1.call-update
  908.1 274.9 %all-reduce.8.cloned.1.call-done = f32[512,4608]{1,0:T(8,128)} async-done(((f32[512,4608]{1,0:T(8,128)}), f32[512,4608]{1,0:T(8,128)}) %all-reduce.8.cloned.1.call-update) | async-done | bytes 9437200
  1183.0 0.0 copy-done.4
  1183.0 0.0 copy-done.5
  1183.0 1.6 multiply_reduce_fusion.1
  1184.6 4.6 stack.2
  1189.2 11.2 all-to-all-start
  1200.4 146.5 %all-reduce.2 = (f32[]{:T(128)}, f32[]{:T(128)}) all-reduce(f32[]{:T(128)} %get-tuple-element.9, f32[]{:T(128)} %get-tuple-element.5), channel_id=1, replica_groups=mesh['dp'=16,'fsdp'=16] {'dp','fsdp'}, use_global_device_ids=true, to_apply=%region_8.0 | all-reduce | flops 2 | bytes 16 | tf_op jit(solution)/shard_map/psum | solution.py:42
  1348.2 0.0 all-to-all-done
  1348.2 0.0 slice-start
  1348.2 7.7 reshape.42
  1355.9 0.0 copy-start.2
  1355.9 0.0 copy-start.3
  1355.9 0.0 slice-start.1
  1355.9 5.2 fusion.9
  1361.1 0.0 copy-done.2
  1361.1 0.0 copy-done.3
  1361.1 2.9 fusion
  1364.0 0.0 slice-done
  1364.0 0.0 slice-done.1
  1364.0 2.9 convolution_convert_fusion
  1366.8 3.3 convert_reduce_fusion
  (4 shorter events, 0.0 us)
Async XLA Ops:
  7.2 1.7 copy-start
  7.2 150.2 %all-reduce.6.cloned.1.call-start = ((), (), s32[]{:S(2)}) async-start(), calls=%async_computation.2 | async-start | bytes 1179648
  10.9 879.3 %all-gather.3.cloned.1.call-start = ((), (), s32[]{:S(2)}) async-start(), calls=%async_computation.1 | async-start | bytes 4737024 | tf_op jit(solution)/shard_map/all_gather | solution.py:25
  160.1 1023.0 %all-reduce.8.cloned.1.call-start = ((), (), s32[]{:S(2)}) async-start(), calls=%async_computation.3 | async-start | bytes 18874368
  162.3 735.4 %copy-start.6 = (f32[256]{0:T(256)S(1)}, f32[256]{0:T(256)}, u32[]{:S(2)}) copy-start(f32[256]{0:T(256)} %param.13) | copy-start | bytes 3076
  897.8 5.2 copy-start.1
  908.1 275.0 %copy-start.4 = (bf16[2,4608]{1,0:T(2,128)(2,1)S(1)}, bf16[2,4608]{1,0:T(2,128)(2,1)}, u32[]{:S(2)}) copy-start(bf16[2,4608]{1,0:T(2,128)(2,1)} %add_convert_fusion) | copy-start | bytes 55300
  908.1 275.0 %copy-start.5 = (f32[4608]{0:T(1024)S(1)}, f32[4608]{0:T(1024)}, u32[]{:S(2)}) copy-start(f32[4608]{0:T(1024)} %param.15) | copy-start | bytes 55300
  1189.2 159.0 %all-to-all-start = ((bf16[256,2,4608]{2,1,0:T(2,128)(2,1)}), bf16[256,2,4608]{2,1,0:T(2,128)(2,1)}, u32[]{:S(2)}, u32[]{:S(2)}) async-start(bf16[256,2,4608]{2,1,0:T(2,128)(2,1)} %stack.2), calls=%async_computation | async-start | bytes 9437184 | tf_op jit(solution)/shard_map/all_to_all | solution.py:48
  1348.2 15.8 %slice-start = ((s8[4718592]{0:T(1024)(128)(4,1)}), s8[524288]{0:T(1024)(128)(4,1)S(1)}, s32[]{:S(2)}) async-start(s8[4718592]{0:T(1024)(128)(4,1)} %bitcast.12), calls=%async_computation.4 | async-start | bytes 1048576
  1355.9 5.2 copy-start.2
  1355.9 5.2 copy-start.3
  1355.9 8.1 slice-start.1
Sparse Core Ops, SparseCore 0:
  11.2 146.0 all-reduce.5
  160.2 729.9 all-gather.2
  908.2 274.7 all-reduce.7
